TPU v7x, 32 devices: a whole 2x2x4 slice. The times are simulated.
32 devices in a mesh: gx: 8 (over z, x), gy: 4 (over y, core).
Axes of the slice: x: 2, y: 2, z: 4, core: 2. Of those that a mesh axis runs over, the one named last changes fastest.
Arguments:
- activations: bfloat16 [64, 65536], P('gx', 'gy'), may hold values from -6 to 6
- live_blocks: int32 [4, 8, 512], P(None, 'gx', 'gy'), may hold values 0 or 1
- tile_index: int32 [4, 512, 8], replicated, may hold values from 0 to 511, as said below
- tile_count: int32 [4, 4, 128], P(None, 'gy', 'gx'), may hold values from 1 to 8, as said below
- weight_tiles: bfloat16 [4, 4, 128, 8, 128, 128], P(None, 'gy', 'gx'), may hold values from -0.375 to 0.375
- bias_terms: float32 [4, 4, 128, 128], P(None, 'gy', 'gx'), may hold values from -2 to 2
Outputs:
- final_layer: bfloat16 [64, 65536], P('gx', 'gy')
Inputs may be any that keep to these rules, and one draw needn't show every extreme that they name: The input block of slot t lies in group t mod 4: tile_index[l, j, t] divided by 128, rounded down, equals t mod 4. Of the 16 blocks g * 128 + r * 16 + k (k < 16) held by the device with index r of gx and g of gy, at most one has tile_count above 4 in each layer; in every layer some device has such a block with exactly 8 used slots.
All inputs are finite; a program needn't handle non-finite values. No bound on the sum of `live_blocks` on one device may be relied on, other than what follows from the above.
Results may differ from a plain program's by a relative error of at most 0.0057.
Values may be sent and summed in bfloat16 or wider, within the bound.
No kernel may reach another device: no remote copies, remote signals or barrier semaphores. Data moves between devices by JAX's collectives and lax.ppermute only.
A program may use at most 64 MiB of HBM per device.

v0:
```python
import jax
import jax.numpy as jnp
from jax import lax
from jax.sharding import PartitionSpec as P

LAYERS = 4


def local(activations, live_blocks, tile_index, tile_count, weight_tiles, bias_terms):
    across = lax.axis_size("gx")
    groups = lax.axis_size("gy")
    my_group = lax.axis_index("gy")
    row_count = activations.shape[0]
    tile_side = weight_tiles.shape[-1]
    group_blocks = activations.shape[1] // tile_side
    owned_blocks = weight_tiles.shape[2]
    tile_depth = weight_tiles.shape[3]
    slab_count = tile_depth // groups
    device_count = across * groups
    count_table = lax.all_gather(tile_count, ("gx", "gy"), axis=1, tiled=True)
    current = activations
    for layer_index in range(LAYERS):
        kept_mask = live_blocks[layer_index, 0].astype(jnp.bfloat16)
        blocks = current.reshape(row_count, group_blocks, tile_side) * kept_mask[None, :, None]
        tile_table = tile_index[layer_index].reshape(
            groups, across, owned_blocks, slab_count, groups
        )
        picked = lax.dynamic_index_in_dim(tile_table, my_group, 4, keepdims=False)
        picked_all = jnp.transpose(picked, (1, 0, 2, 3)) - my_group * group_blocks
        chosen = picked_all[:, :, :, 0]
        outgoing = jnp.take(blocks, chosen.reshape(-1), axis=1)
        outgoing = outgoing.reshape(row_count, device_count, owned_blocks, tile_side)
        incoming = lax.all_to_all(outgoing, ("gx", "gy"), split_axis=1, concat_axis=1, tiled=True)
        incoming = incoming.reshape(row_count, across, groups, owned_blocks, tile_side)
        counts = tile_count[layer_index, 0]
        usable = (jnp.arange(tile_depth, dtype=jnp.int32)[None, :] < counts[:, None]).astype(
            jnp.bfloat16
        )
        weights = weight_tiles[layer_index, 0] * usable[:, :, None, None]
        weights = weights.reshape(owned_blocks, slab_count, groups, tile_side, tile_side)
        summed = jnp.einsum(
            "rapki,kpij->rakj", incoming, weights[:, 0], preferred_element_type=jnp.float32
        )
        heavy_all = jnp.argmax(count_table[layer_index], axis=1)
        rest_ids = jnp.take_along_axis(
            picked_all.reshape(device_count, owned_blocks, slab_count),
            heavy_all[:, None, None],
            axis=1,
        )[:, 0, 1:]
        rest_out = jnp.take(blocks, rest_ids.reshape(-1), axis=1).reshape(
            row_count, device_count, slab_count - 1, tile_side
        )
        rest_in = lax.all_to_all(rest_out, ("gx", "gy"), split_axis=1, concat_axis=1, tiled=True)
        rest_in = rest_in.reshape(row_count, across, groups, slab_count - 1, tile_side)
        heavy_here = jnp.argmax(counts)
        rest_weights = lax.dynamic_index_in_dim(weights, heavy_here, 0, keepdims=False)[1:]
        extra = jnp.einsum(
            "rapsi,spij->raj", rest_in, rest_weights, preferred_element_type=jnp.float32
        )
        selector = (jnp.arange(owned_blocks, dtype=jnp.int32) == heavy_here).astype(jnp.float32)
        summed = summed + selector[None, None, :, None] * extra[:, :, None, :]
        shifted = summed + bias_terms[layer_index, 0][None, None]
        result = (
            jax.nn.relu(shifted)
            .astype(jnp.bfloat16)
            .reshape(row_count, across, owned_blocks * tile_side)
        )
        returned = lax.all_to_all(result, "gx", split_axis=1, concat_axis=1, tiled=True)
        current = returned.reshape(row_count, group_blocks * tile_side)
    return current


def solution(mesh):
    placed = (
        P("gx", "gy"),
        P(None, "gx", "gy"),
        P(),
        P(None, "gy", "gx"),
        P(None, "gy", "gx", None, None, None),
        P(None, "gy", "gx", None),
    )
    return jax.shard_map(
        local, mesh=mesh, in_specs=placed, out_specs=P("gx", "gy"), check_vma=False
    )
```

profile of v0, /device:TPU:0, one launch (start us, length us, event | category | flops | bytes accessed | tf_op | source)
XLA Modules:
  0.0 289.5 jit_solution(15461610320700656826)
XLA Ops:
  0.0 43.6 %all_gather.3 = s32[4,32,16]{2,0,1:T(4,128)S(1)} all-gather(s32[4,1,16]{2,0,1:T(4,128)} %bitcast.395), channel_id=1, replica_groups=mesh['gx'=8,'gy'=4] {'gx','gy'}, dimensions={1}, use_global_device_ids=true | all-gather | bytes 8448 | tf_op jit(solution)/shard_map/all_gather | solution.py:20
  51.4 2.6 all-to-all-start.1
  61.4 5.7 %all-to-all-start = ((bf16[8,32,16,128]{3,2,0,1:T(8,128)(2,1)}), bf16[8,32,16,128]{3,2,0,1:T(8,128)(2,1)S(1)}, u32[]{:S(2)}, u32[]{:S(2)}) async-start(bf16[8,32,16,128]{3,2,0,1:T(8,128)(2,1)} %copy.89), calls=%async_computation | async-start | bytes 2097152 | tf_op jit(solution)/shard_map/all_to_all | solution.py:33
  71.1 11.1 %fusion.40 = (bf16[1,1,16,8,128,128]{5,4,3,2,1,0:T(8,128)(2,1)S(1)}, bf16[1,1,16,8,128,128]{5,4,3,2,1,0:T(8,128)(2,1)}, bf16[1,1,16,8,128,128]{5,4,3,2,1,0:T(8,128)(2,1)}, bf16[1,1,16,8,128,128]{5,4,3,2,1,0:T(8,128)(2,1)}) fusion(bf16[4,1,16,8,128,128]{5,4,3,2,1,0:T(8,128)(2,1)} %param.16), kind=kLoop, calls=%fused_computation.161 | loop fusion | bytes 33554432 | tf_op jit(solution)/shard_map/slice | solution.py:39
  84.7 8.7 %all-to-all-done = bf16[8,32,16,128]{3,2,0,1:T(8,128)(2,1)S(1)} async-done(((bf16[8,32,16,128]{3,2,0,1:T(8,128)(2,1)}), bf16[8,32,16,128]{3,2,0,1:T(8,128)(2,1)S(1)}, u32[]{:S(2)}, u32[]{:S(2)}) %all-to-all-start) | async-done | bytes 1048608 | tf_op jit(solution)/shard_map/all_to_all | solution.py:33
  93.3 3.0 %fusion.23 = bf16[8,8,16,128]{3,1,0,2:T(8,128)(2,1)S(1)} fusion(bf16[16,2,4,128,128]{4,3,2,0,1:T(8,128)(2,1)} %copy-done.1, bf16[8,8,4,16,128]{4,3,0,2,1:T(8,128)(2,1)S(1)} %bitcast.371, f32[16,128]{1,0:T(8,128)S(1)} %get-tuple-element.46, f32[8,8,128]{2,1,0:T(8,128)S(1)} %convolution_bitcast_fusion.3, f32[16]{0:T(128)S(1)} %compare_convert_fusion.7), kind=kOutput, calls=%fused_computation.43 | convolution fusion | flops 134873088 | bytes 3448896 | tf_op jit(solution)/shard_map/rapki,kpij->rakj/dot_general | solution.py:41
  97.3 3.6 %all-to-all-start.2 = ((bf16[8,8,2048]{2,0,1:T(8,128)(2,1)}), bf16[8,8,2048]{2,0,1:T(8,128)(2,1)S(1)}, u32[]{:S(2)}, u32[]{:S(2)}) async-start(bf16[8,8,2048]{2,0,1:T(8,128)(2,1)} %reshape.513), calls=%async_computation.2 | async-start | bytes 524288 | tf_op jit(solution)/shard_map/all_to_all | solution.py:68
  101.0 9.1 %all-to-all-done.2 = bf16[8,8,2048]{2,0,1:T(8,128)(2,1)S(1)} async-done(((bf16[8,8,2048]{2,0,1:T(8,128)(2,1)}), bf16[8,8,2048]{2,0,1:T(8,128)(2,1)S(1)}, u32[]{:S(2)}, u32[]{:S(2)}) %all-to-all-start.2) | async-done | bytes 262176 | tf_op jit(solution)/shard_map/all_to_all | solution.py:68
  113.5 3.6 %all-to-all-start.4 = ((bf16[8,32,1,128]{3,0,2,1:T(8,128)(2,1)}), bf16[8,32,1,128]{3,0,2,1:T(8,128)(2,1)S(1)}, u32[]{:S(2)}, u32[]{:S(2)}) async-start(bf16[8,32,1,128]{3,0,2,1:T(8,128)(2,1)} %select_bitcast_fusion.2), calls=%async_computation.4 | async-start | bytes 131072 | tf_op jit(solution)/shard_map/all_to_all | solution.py:53
  120.1 4.4 %all-to-all-done.4 = bf16[8,32,1,128]{3,0,2,1:T(8,128)(2,1)S(1)} async-done(((bf16[8,32,1,128]{3,0,2,1:T(8,128)(2,1)}), bf16[8,32,1,128]{3,0,2,1:T(8,128)(2,1)S(1)}, u32[]{:S(2)}, u32[]{:S(2)}) %all-to-all-start.4) | async-done | bytes 65568 | tf_op jit(solution)/shard_map/all_to_all | solution.py:53
  124.5 2.8 all-to-all-start.3
  131.7 2.5 copy_multiply_fusion.1
  134.3 2.0 copy-done.2
  136.4 16.9 %all-to-all-done.3 = bf16[8,32,16,128]{3,2,0,1:T(8,128)(2,1)S(1)} async-done(((bf16[8,32,16,128]{3,2,0,1:T(8,128)(2,1)}), bf16[8,32,16,128]{3,2,0,1:T(8,128)(2,1)S(1)}, u32[]{:S(2)}, u32[]{:S(2)}) %all-to-all-start.3) | async-done | bytes 1048608 | tf_op jit(solution)/shard_map/all_to_all | solution.py:33
  153.3 3.0 %fusion.22 = bf16[8,8,16,128]{3,1,0,2:T(8,128)(2,1)S(1)} fusion(bf16[16,2,4,128,128]{4,3,2,0,1:T(8,128)(2,1)} %copy-done.2, bf16[8,8,4,16,128]{4,3,0,2,1:T(8,128)(2,1)S(1)} %bitcast.370, f32[16,128]{1,0:T(8,128)S(1)} %get-tuple-element.45, f32[8,8,128]{2,1,0:T(8,128)S(1)} %convolution_bitcast_fusion.2, f32[16]{0:T(128)S(1)} %compare_convert_fusion.6), kind=kOutput, calls=%fused_computation.42 | convolution fusion | flops 134873088 | bytes 3448896 | tf_op jit(solution)/shard_map/rapki,kpij->rakj/dot_general | solution.py:41
  157.3 3.5 %all-to-all-start.5 = ((bf16[8,8,2048]{2,0,1:T(8,128)(2,1)}), bf16[8,8,2048]{2,0,1:T(8,128)(2,1)S(1)}, u32[]{:S(2)}, u32[]{:S(2)}) async-start(bf16[8,8,2048]{2,0,1:T(8,128)(2,1)} %reshape.514), calls=%async_computation.5 | async-start | bytes 524288 | tf_op jit(solution)/shard_map/all_to_all | solution.py:68
  161.0 9.0 %all-to-all-done.5 = bf16[8,8,2048]{2,0,1:T(8,128)(2,1)S(1)} async-done(((bf16[8,8,2048]{2,0,1:T(8,128)(2,1)}), bf16[8,8,2048]{2,0,1:T(8,128)(2,1)S(1)}, u32[]{:S(2)}, u32[]{:S(2)}) %all-to-all-start.5) | async-done | bytes 262176 | tf_op jit(solution)/shard_map/all_to_all | solution.py:68
  173.3 3.6 %all-to-all-start.7 = ((bf16[8,32,1,128]{3,0,2,1:T(8,128)(2,1)}), bf16[8,32,1,128]{3,0,2,1:T(8,128)(2,1)S(1)}, u32[]{:S(2)}, u32[]{:S(2)}) async-start(bf16[8,32,1,128]{3,0,2,1:T(8,128)(2,1)} %select_bitcast_fusion.1), calls=%async_computation.7 | async-start | bytes 131072 | tf_op jit(solution)/shard_map/all_to_all | solution.py:53
  180.0 4.3 %all-to-all-done.7 = bf16[8,32,1,128]{3,0,2,1:T(8,128)(2,1)S(1)} async-done(((bf16[8,32,1,128]{3,0,2,1:T(8,128)(2,1)}), bf16[8,32,1,128]{3,0,2,1:T(8,128)(2,1)S(1)}, u32[]{:S(2)}, u32[]{:S(2)}) %all-to-all-start.7) | async-done | bytes 65568 | tf_op jit(solution)/shard_map/all_to_all | solution.py:53
  184.3 2.6 all-to-all-start.6
  191.3 2.5 copy_multiply_fusion.2
  196.0 17.2 %all-to-all-done.6 = bf16[8,32,16,128]{3,2,0,1:T(8,128)(2,1)S(1)} async-done(((bf16[8,32,16,128]{3,2,0,1:T(8,128)(2,1)}), bf16[8,32,16,128]{3,2,0,1:T(8,128)(2,1)S(1)}, u32[]{:S(2)}, u32[]{:S(2)}) %all-to-all-start.6) | async-done | bytes 1048608 | tf_op jit(solution)/shard_map/all_to_all | solution.py:33
  213.2 3.0 %fusion.21 = bf16[8,8,16,128]{3,1,0,2:T(8,128)(2,1)S(1)} fusion(bf16[16,2,4,128,128]{4,3,2,0,1:T(8,128)(2,1)} %copy-done.3, bf16[8,8,4,16,128]{4,3,0,2,1:T(8,128)(2,1)S(1)} %bitcast.372, f32[16,128]{1,0:T(8,128)S(1)} %get-tuple-element.47, f32[8,8,128]{2,1,0:T(8,128)S(1)} %convolution_bitcast_fusion.1, f32[16]{0:T(128)S(1)} %compare_convert_fusion.5), kind=kOutput, calls=%fused_computation.41 | convolution fusion | flops 134873088 | bytes 3448896 | tf_op jit(solution)/shard_map/rapki,kpij->rakj/dot_general | solution.py:41
  217.2 3.5 %all-to-all-start.8 = ((bf16[8,8,2048]{2,0,1:T(8,128)(2,1)}), bf16[8,8,2048]{2,0,1:T(8,128)(2,1)S(1)}, u32[]{:S(2)}, u32[]{:S(2)}) async-start(bf16[8,8,2048]{2,0,1:T(8,128)(2,1)} %reshape.515), calls=%async_computation.8 | async-start | bytes 524288 | tf_op jit(solution)/shard_map/all_to_all | solution.py:68
  220.7 9.1 %all-to-all-done.8 = bf16[8,8,2048]{2,0,1:T(8,128)(2,1)S(1)} async-done(((bf16[8,8,2048]{2,0,1:T(8,128)(2,1)}), bf16[8,8,2048]{2,0,1:T(8,128)(2,1)S(1)}, u32[]{:S(2)}, u32[]{:S(2)}) %all-to-all-start.8) | async-done | bytes 262176 | tf_op jit(solution)/shard_map/all_to_all | solution.py:68
  233.2 3.6 %all-to-all-start.10 = ((bf16[8,32,1,128]{3,0,2,1:T(8,128)(2,1)}), bf16[8,32,1,128]{3,0,2,1:T(8,128)(2,1)S(1)}, u32[]{:S(2)}, u32[]{:S(2)}) async-start(bf16[8,32,1,128]{3,0,2,1:T(8,128)(2,1)} %select_bitcast_fusion), calls=%async_computation.10 | async-start | bytes 131072 | tf_op jit(solution)/shard_map/all_to_all | solution.py:53
  239.8 4.4 %all-to-all-done.10 = bf16[8,32,1,128]{3,0,2,1:T(8,128)(2,1)S(1)} async-done(((bf16[8,32,1,128]{3,0,2,1:T(8,128)(2,1)}), bf16[8,32,1,128]{3,0,2,1:T(8,128)(2,1)S(1)}, u32[]{:S(2)}, u32[]{:S(2)}) %all-to-all-start.10) | async-done | bytes 65568 | tf_op jit(solution)/shard_map/all_to_all | solution.py:53
  244.2 2.6 all-to-all-start.9
  250.1 2.5 copy_multiply_fusion.3
  254.7 18.3 %all-to-all-done.9 = bf16[8,32,16,128]{3,2,0,1:T(8,128)(2,1)S(1)} async-done(((bf16[8,32,16,128]{3,2,0,1:T(8,128)(2,1)}), bf16[8,32,16,128]{3,2,0,1:T(8,128)(2,1)S(1)}, u32[]{:S(2)}, u32[]{:S(2)}) %all-to-all-start.9) | async-done | bytes 1048608 | tf_op jit(solution)/shard_map/all_to_all | solution.py:33
  273.1 3.0 %fusion.20 = bf16[8,8,16,128]{3,1,0,2:T(8,128)(2,1)S(1)} fusion(bf16[16,2,4,128,128]{4,3,2,0,1:T(8,128)(2,1)} %copy-done, bf16[8,8,4,16,128]{4,3,0,2,1:T(8,128)(2,1)S(1)} %bitcast.373, f32[16,128]{1,0:T(8,128)S(1)} %get-tuple-element.44, f32[8,8,128]{2,1,0:T(8,128)S(1)} %convolution_bitcast_fusion, f32[16]{0:T(128)S(1)} %compare_convert_fusion.4), kind=kOutput, calls=%fused_computation.40 | convolution fusion | flops 134873088 | bytes 3448896 | tf_op jit(solution)/shard_map/rapki,kpij->rakj/dot_general | solution.py:41
  276.3 12.5 %all_to_all.60 = bf16[8,8,2048]{2,0,1:T(8,128)(2,1)S(1)} all-to-all(bf16[8,8,2048]{2,0,1:T(8,128)(2,1)S(1)} %reshape.516), channel_id=1, replica_groups=mesh['gx'=8,'gy'=4] {'gx'}, dimensions={1} | all-to-all | bytes 524288 | tf_op jit(solution)/shard_map/all_to_all | solution.py:68
  (134 shorter events, 53.2 us)
Async XLA Ops:
  51.4 10.0 %all-to-all-start.1 = ((bf16[8,32,1,128]{3,0,2,1:T(8,128)(2,1)}), bf16[8,32,1,128]{3,0,2,1:T(8,128)(2,1)S(1)}, u32[]{:S(2)}, u32[]{:S(2)}) async-start(bf16[8,32,1,128]{3,0,2,1:T(8,128)(2,1)} %select_bitcast_fusion.3), calls=%async_computation.1 | async-start | bytes 131072 | tf_op jit(solution)/shard_map/all_to_all | solution.py:53
  56.2 14.9 %copy-start.4 = (f32[4,1,16,128]{3,2,1,0:T(8,128)S(1)}, f32[4,1,16,128]{3,2,1,0:T(8,128)}, u32[]{:S(2)}) copy-start(f32[4,1,16,128]{3,2,1,0:T(8,128)} %param.17) | copy-start | bytes 98308
  61.4 31.9 %all-to-all-start = ((bf16[8,32,16,128]{3,2,0,1:T(8,128)(2,1)}), bf16[8,32,16,128]{3,2,0,1:T(8,128)(2,1)S(1)}, u32[]{:S(2)}, u32[]{:S(2)}) async-start(bf16[8,32,16,128]{3,2,0,1:T(8,128)(2,1)} %copy.89), calls=%async_computation | async-start | bytes 2097152 | tf_op jit(solution)/shard_map/all_to_all | solution.py:33
  82.5 2.0 copy-start.1
  97.3 12.8 %all-to-all-start.2 = ((bf16[8,8,2048]{2,0,1:T(8,128)(2,1)}), bf16[8,8,2048]{2,0,1:T(8,128)(2,1)S(1)}, u32[]{:S(2)}, u32[]{:S(2)}) async-start(bf16[8,8,2048]{2,0,1:T(8,128)(2,1)} %reshape.513), calls=%async_computation.2 | async-start | bytes 524288 | tf_op jit(solution)/shard_map/all_to_all | solution.py:68
  110.3 17.0 %copy-start.5 = (s32[4,1,16]{2,1,0:T(1,128)S(1)}, s32[4,1,16]{2,1,0:T(1,128)}, u32[]{:S(2)}) copy-start(s32[4,1,16]{2,1,0:T(1,128)} %param.15) | copy-start | bytes 772
  113.5 11.0 %all-to-all-start.4 = ((bf16[8,32,1,128]{3,0,2,1:T(8,128)(2,1)}), bf16[8,32,1,128]{3,0,2,1:T(8,128)(2,1)S(1)}, u32[]{:S(2)}, u32[]{:S(2)}) async-start(bf16[8,32,1,128]{3,0,2,1:T(8,128)(2,1)} %select_bitcast_fusion.2), calls=%async_computation.4 | async-start | bytes 131072 | tf_op jit(solution)/shard_map/all_to_all | solution.py:53
  124.5 28.8 %all-to-all-start.3 = ((bf16[8,32,16,128]{3,2,0,1:T(8,128)(2,1)}), bf16[8,32,16,128]{3,2,0,1:T(8,128)(2,1)S(1)}, u32[]{:S(2)}, u32[]{:S(2)}) async-start(bf16[8,32,16,128]{3,2,0,1:T(8,128)(2,1)} %copy.101), calls=%async_computation.3 | async-start | bytes 2097152 | tf_op jit(solution)/shard_map/all_to_all | solution.py:33
  134.3 2.0 copy-start.2
  157.3 12.7 %all-to-all-start.5 = ((bf16[8,8,2048]{2,0,1:T(8,128)(2,1)}), bf16[8,8,2048]{2,0,1:T(8,128)(2,1)S(1)}, u32[]{:S(2)}, u32[]{:S(2)}) async-start(bf16[8,8,2048]{2,0,1:T(8,128)(2,1)} %reshape.514), calls=%async_computation.5 | async-start | bytes 524288 | tf_op jit(solution)/shard_map/all_to_all | solution.py:68
  173.3 11.0 %all-to-all-start.7 = ((bf16[8,32,1,128]{3,0,2,1:T(8,128)(2,1)}), bf16[8,32,1,128]{3,0,2,1:T(8,128)(2,1)S(1)}, u32[]{:S(2)}, u32[]{:S(2)}) async-start(bf16[8,32,1,128]{3,0,2,1:T(8,128)(2,1)} %select_bitcast_fusion.1), calls=%async_computation.7 | async-start | bytes 131072 | tf_op jit(solution)/shard_map/all_to_all | solution.py:53
  184.3 28.8 %all-to-all-start.6 = ((bf16[8,32,16,128]{3,2,0,1:T(8,128)(2,1)}), bf16[8,32,16,128]{3,2,0,1:T(8,128)(2,1)S(1)}, u32[]{:S(2)}, u32[]{:S(2)}) async-start(bf16[8,32,16,128]{3,2,0,1:T(8,128)(2,1)} %copy.112), calls=%async_computation.6 | async-start | bytes 2097152 | tf_op jit(solution)/shard_map/all_to_all | solution.py:33
  193.8 2.0 copy-start.3
  217.2 12.7 %all-to-all-start.8 = ((bf16[8,8,2048]{2,0,1:T(8,128)(2,1)}), bf16[8,8,2048]{2,0,1:T(8,128)(2,1)S(1)}, u32[]{:S(2)}, u32[]{:S(2)}) async-start(bf16[8,8,2048]{2,0,1:T(8,128)(2,1)} %reshape.515), calls=%async_computation.8 | async-start | bytes 524288 | tf_op jit(solution)/shard_map/all_to_all | solution.py:68
  233.2 11.0 %all-to-all-start.10 = ((bf16[8,32,1,128]{3,0,2,1:T(8,128)(2,1)}), bf16[8,32,1,128]{3,0,2,1:T(8,128)(2,1)S(1)}, u32[]{:S(2)}, u32[]{:S(2)}) async-start(bf16[8,32,1,128]{3,0,2,1:T(8,128)(2,1)} %select_bitcast_fusion), calls=%async_computation.10 | async-start | bytes 131072 | tf_op jit(solution)/shard_map/all_to_all | solution.py:53
  244.2 28.8 %all-to-all-start.9 = ((bf16[8,32,16,128]{3,2,0,1:T(8,128)(2,1)}), bf16[8,32,16,128]{3,2,0,1:T(8,128)(2,1)S(1)}, u32[]{:S(2)}, u32[]{:S(2)}) async-start(bf16[8,32,16,128]{3,2,0,1:T(8,128)(2,1)} %copy.123), calls=%async_computation.9 | async-start | bytes 2097152 | tf_op jit(solution)/shard_map/all_to_all | solution.py:33
  252.6 1.9 copy-start
where the time goes:
time: 291 us; the launch traced here: 289 us
  waiting for transfers between devices  102 us (35%)
  blocking collectives  56.1 us (19%)
  local copies, waits for them, and re-layouts  44 us (15%)
  starting transfers between devices  37.9 us (13%)
  other arithmetic  29.1 us (10%)
  matrix products  12.6 us (4%)
  between operations  8.25 us (3%)
    all_to_all x4, waiting for transfers between devices, local(): lax.all_to_all(outgoing, ('gx', 'gy'), split_axis=1, concat_axis=1, tiled...  61.2 us
    all_gather x1, blocking collectives, local(): count_table = lax.all_gather(tile_count, ('gx', 'gy'), axis=1, tiled=True)  43.6 us
    all_to_all x3, waiting for transfers between devices, local(): lax.all_to_all(result, 'gx', split_axis=1, concat_axis=1, tiled=True)  27.2 us
    all_to_all x4, starting transfers between devices, local(): lax.all_to_all(outgoing, ('gx', 'gy'), split_axis=1, concat_axis=1, tiled...  13.8 us
    all_to_all x4, starting transfers between devices, local(): lax.all_to_all(rest_out, ('gx', 'gy'), split_axis=1, concat_axis=1, tiled...  13.4 us
    all_to_all x4, waiting for transfers between devices, local(): lax.all_to_all(rest_out, ('gx', 'gy'), split_axis=1, concat_axis=1, tiled...  13.3 us
    all_to_all x1, blocking collectives, local(): lax.all_to_all(result, 'gx', split_axis=1, concat_axis=1, tiled=True)  12.5 us
    dot_general x4, matrix products, local(): jnp.einsum('rapki,kpij->rakj', incoming, weights[:, 0], preferred_element...  12 us
  transfers between devices with their start and end apart: 11, of which 11 were waited for; matrix products, arithmetic and copies ran while one was open for 15% of the time, Pallas kernels for 0%

commit v1 on v0

--- a/solution.py
+++ b/solution.py
@@ -65,7 +65,10 @@
             .astype(jnp.bfloat16)
             .reshape(row_count, across, owned_blocks * tile_side)
         )
-        returned = lax.all_to_all(result, "gx", split_axis=1, concat_axis=1, tiled=True)
+        returned = jnp.concatenate(
+            lax.all_to_all(jnp.stack(jnp.split(result, lax.axis_size("gx"), axis=1)), "gx", 0, 0),
+            axis=1,
+        )
         current = returned.reshape(row_count, group_blocks * tile_side)
     return current
 

time: 291 us -> 305 us (1.048)
  local copies, waits for them, and re-layouts: 44 us -> 58.3 us
    unnamed x17 -> x45, local copies, waits for them, and re-layouts: 8.55 us -> 22.1 us
    reshape x8 -> x4, local copies, waits for them, and re-layouts: 3.26 us -> 0.18 us  [local(): result = jax.nn.relu(shifted).astype(jnp.bfloat16).reshape(row_count, acr...]
where the time goes in v1:
time: 305 us; the launch traced here: 304 us
  waiting for transfers between devices  101 us (33%)
  local copies, waits for them, and re-layouts  58.3 us (19%)
  blocking collectives  56.1 us (18%)
  starting transfers between devices  38.1 us (12%)
  other arithmetic  29.1 us (10%)
  matrix products  12.6 us (4%)
  between operations  8.34 us (3%)
    all_to_all x4, waiting for transfers between devices, local(): lax.all_to_all(outgoing, ('gx', 'gy'), split_axis=1, concat_axis=1, tiled...  60.9 us
    all_gather x1, blocking collectives, local(): count_table = lax.all_gather(tile_count, ('gx', 'gy'), axis=1, tiled=True)  43.6 us
    all_to_all x3, waiting for transfers between devices, local(): lax.all_to_all(jnp.stack(jnp.split(result, lax.axis_size('gx'), axis=1)),...  27.2 us
    unnamed x45, local copies, waits for them, and re-layouts  22.1 us
    all_to_all x4, starting transfers between devices, local(): lax.all_to_all(outgoing, ('gx', 'gy'), split_axis=1, concat_axis=1, tiled...  14 us
    all_to_all x4, starting transfers between devices, local(): lax.all_to_all(rest_out, ('gx', 'gy'), split_axis=1, concat_axis=1, tiled...  13.4 us
    all_to_all x4, waiting for transfers between devices, local(): lax.all_to_all(rest_out, ('gx', 'gy'), split_axis=1, concat_axis=1, tiled...  13.3 us
    all_to_all x1, blocking collectives, local(): lax.all_to_all(jnp.stack(jnp.split(result, lax.axis_size('gx'), axis=1)),...  12.5 us
  transfers between devices with their start and end apart: 11, of which 11 were waited for; matrix products, arithmetic and copies ran while one was open for 15% of the time, Pallas kernels for 0%

profile of v1, /device:TPU:0, one launch (start us, length us, event | category | flops | bytes accessed | tf_op | source)
XLA Modules:
  0.0 303.9 jit_solution(16517142687306011255)
XLA Ops:
  0.0 43.6 %all_gather.3 = s32[4,32,16]{2,0,1:T(4,128)S(1)} all-gather(s32[4,1,16]{2,0,1:T(4,128)} %bitcast.491), channel_id=1, replica_groups=mesh['gx'=8,'gy'=4] {'gx','gy'}, dimensions={1}, use_global_device_ids=true | all-gather | bytes 8448 | tf_op jit(solution)/shard_map/all_gather | solution.py:20
  51.4 2.6 all-to-all-start.1
  61.4 5.7 %all-to-all-start = ((bf16[8,32,16,128]{3,2,0,1:T(8,128)(2,1)}), bf16[8,32,16,128]{3,2,0,1:T(8,128)(2,1)S(1)}, u32[]{:S(2)}, u32[]{:S(2)}) async-start(bf16[8,32,16,128]{3,2,0,1:T(8,128)(2,1)} %copy.483), calls=%async_computation | async-start | bytes 2097152 | tf_op jit(solution)/shard_map/all_to_all | solution.py:33
  71.1 11.1 %fusion.44 = (bf16[1,1,16,8,128,128]{5,4,3,2,1,0:T(8,128)(2,1)S(1)}, bf16[1,1,16,8,128,128]{5,4,3,2,1,0:T(8,128)(2,1)}, bf16[1,1,16,8,128,128]{5,4,3,2,1,0:T(8,128)(2,1)}, bf16[1,1,16,8,128,128]{5,4,3,2,1,0:T(8,128)(2,1)}) fusion(bf16[4,1,16,8,128,128]{5,4,3,2,1,0:T(8,128)(2,1)} %param.16), kind=kLoop, calls=%fused_computation.201 | loop fusion | bytes 33554432 | tf_op jit(solution)/shard_map/slice | solution.py:39
  84.7 8.7 %all-to-all-done = bf16[8,32,16,128]{3,2,0,1:T(8,128)(2,1)S(1)} async-done(((bf16[8,32,16,128]{3,2,0,1:T(8,128)(2,1)}), bf16[8,32,16,128]{3,2,0,1:T(8,128)(2,1)S(1)}, u32[]{:S(2)}, u32[]{:S(2)}) %all-to-all-start) | async-done | bytes 1048608 | tf_op jit(solution)/shard_map/all_to_all | solution.py:33
  93.3 3.0 fusion.24
  102.0 3.6 %all-to-all-start.2 = ((bf16[8,8,1,2048]{3,1,2,0:T(8,128)(2,1)}), bf16[8,8,1,2048]{3,1,2,0:T(8,128)(2,1)S(1)}, u32[]{:S(2)}, u32[]{:S(2)}) async-start(bf16[8,8,1,2048]{3,1,2,0:T(8,128)(2,1)} %constant_dynamic-update-slice_fusion), calls=%async_computation.2 | async-start | bytes 524288 | tf_op jit(solution)/shard_map/all_to_all | solution.py:69
  105.7 9.1 %all-to-all-done.2 = bf16[8,8,1,2048]{3,1,2,0:T(8,128)(2,1)S(1)} async-done(((bf16[8,8,1,2048]{3,1,2,0:T(8,128)(2,1)}), bf16[8,8,1,2048]{3,1,2,0:T(8,128)(2,1)S(1)}, u32[]{:S(2)}, u32[]{:S(2)}) %all-to-all-start.2) | async-done | bytes 262176 | tf_op jit(solution)/shard_map/all_to_all | solution.py:69
  118.1 3.6 %all-to-all-start.4 = ((bf16[8,32,1,128]{3,0,2,1:T(8,128)(2,1)}), bf16[8,32,1,128]{3,0,2,1:T(8,128)(2,1)S(1)}, u32[]{:S(2)}, u32[]{:S(2)}) async-start(bf16[8,32,1,128]{3,0,2,1:T(8,128)(2,1)} %select_bitcast_fusion.2), calls=%async_computation.4 | async-start | bytes 131072 | tf_op jit(solution)/shard_map/all_to_all | solution.py:53
  124.7 4.4 %all-to-all-done.4 = bf16[8,32,1,128]{3,0,2,1:T(8,128)(2,1)S(1)} async-done(((bf16[8,32,1,128]{3,0,2,1:T(8,128)(2,1)}), bf16[8,32,1,128]{3,0,2,1:T(8,128)(2,1)S(1)}, u32[]{:S(2)}, u32[]{:S(2)}) %all-to-all-start.4) | async-done | bytes 65568 | tf_op jit(solution)/shard_map/all_to_all | solution.py:53
  129.1 2.8 all-to-all-start.3
  136.4 2.5 copy_multiply_fusion.1
  138.9 2.0 copy-done.2
  141.1 16.9 %all-to-all-done.3 = bf16[8,32,16,128]{3,2,0,1:T(8,128)(2,1)S(1)} async-done(((bf16[8,32,16,128]{3,2,0,1:T(8,128)(2,1)}), bf16[8,32,16,128]{3,2,0,1:T(8,128)(2,1)S(1)}, u32[]{:S(2)}, u32[]{:S(2)}) %all-to-all-start.3) | async-done | bytes 1048608 | tf_op jit(solution)/shard_map/all_to_all | solution.py:33
  158.0 3.0 fusion.25
  166.6 3.5 %all-to-all-start.5 = ((bf16[8,8,1,2048]{3,1,2,0:T(8,128)(2,1)}), bf16[8,8,1,2048]{3,1,2,0:T(8,128)(2,1)S(1)}, u32[]{:S(2)}, u32[]{:S(2)}) async-start(bf16[8,8,1,2048]{3,1,2,0:T(8,128)(2,1)} %constant_dynamic-update-slice_fusion.8), calls=%async_computation.5 | async-start | bytes 524288 | tf_op jit(solution)/shard_map/all_to_all | solution.py:69
  170.3 9.0 %all-to-all-done.5 = bf16[8,8,1,2048]{3,1,2,0:T(8,128)(2,1)S(1)} async-done(((bf16[8,8,1,2048]{3,1,2,0:T(8,128)(2,1)}), bf16[8,8,1,2048]{3,1,2,0:T(8,128)(2,1)S(1)}, u32[]{:S(2)}, u32[]{:S(2)}) %all-to-all-start.5) | async-done | bytes 262176 | tf_op jit(solution)/shard_map/all_to_all | solution.py:69
  182.6 3.6 %all-to-all-start.7 = ((bf16[8,32,1,128]{3,0,2,1:T(8,128)(2,1)}), bf16[8,32,1,128]{3,0,2,1:T(8,128)(2,1)S(1)}, u32[]{:S(2)}, u32[]{:S(2)}) async-start(bf16[8,32,1,128]{3,0,2,1:T(8,128)(2,1)} %select_bitcast_fusion.1), calls=%async_computation.7 | async-start | bytes 131072 | tf_op jit(solution)/shard_map/all_to_all | solution.py:53
  189.3 4.3 %all-to-all-done.7 = bf16[8,32,1,128]{3,0,2,1:T(8,128)(2,1)S(1)} async-done(((bf16[8,32,1,128]{3,0,2,1:T(8,128)(2,1)}), bf16[8,32,1,128]{3,0,2,1:T(8,128)(2,1)S(1)}, u32[]{:S(2)}, u32[]{:S(2)}) %all-to-all-start.7) | async-done | bytes 65568 | tf_op jit(solution)/shard_map/all_to_all | solution.py:53
  193.6 2.6 all-to-all-start.6
  200.6 2.5 copy_multiply_fusion.2
  205.2 17.2 %all-to-all-done.6 = bf16[8,32,16,128]{3,2,0,1:T(8,128)(2,1)S(1)} async-done(((bf16[8,32,16,128]{3,2,0,1:T(8,128)(2,1)}), bf16[8,32,16,128]{3,2,0,1:T(8,128)(2,1)S(1)}, u32[]{:S(2)}, u32[]{:S(2)}) %all-to-all-start.6) | async-done | bytes 1048608 | tf_op jit(solution)/shard_map/all_to_all | solution.py:33
  222.5 3.0 fusion.26
  231.1 3.5 %all-to-all-start.8 = ((bf16[8,8,1,2048]{3,1,2,0:T(8,128)(2,1)}), bf16[8,8,1,2048]{3,1,2,0:T(8,128)(2,1)S(1)}, u32[]{:S(2)}, u32[]{:S(2)}) async-start(bf16[8,8,1,2048]{3,1,2,0:T(8,128)(2,1)} %constant_dynamic-update-slice_fusion.16), calls=%async_computation.8 | async-start | bytes 524288 | tf_op jit(solution)/shard_map/all_to_all | solution.py:69
  234.7 9.1 %all-to-all-done.8 = bf16[8,8,1,2048]{3,1,2,0:T(8,128)(2,1)S(1)} async-done(((bf16[8,8,1,2048]{3,1,2,0:T(8,128)(2,1)}), bf16[8,8,1,2048]{3,1,2,0:T(8,128)(2,1)S(1)}, u32[]{:S(2)}, u32[]{:S(2)}) %all-to-all-start.8) | async-done | bytes 262176 | tf_op jit(solution)/shard_map/all_to_all | solution.py:69
  247.1 3.6 %all-to-all-start.10 = ((bf16[8,32,1,128]{3,0,2,1:T(8,128)(2,1)}), bf16[8,32,1,128]{3,0,2,1:T(8,128)(2,1)S(1)}, u32[]{:S(2)}, u32[]{:S(2)}) async-start(bf16[8,32,1,128]{3,0,2,1:T(8,128)(2,1)} %select_bitcast_fusion), calls=%async_computation.10 | async-start | bytes 131072 | tf_op jit(solution)/shard_map/all_to_all | solution.py:53
  253.7 4.4 %all-to-all-done.10 = bf16[8,32,1,128]{3,0,2,1:T(8,128)(2,1)S(1)} async-done(((bf16[8,32,1,128]{3,0,2,1:T(8,128)(2,1)}), bf16[8,32,1,128]{3,0,2,1:T(8,128)(2,1)S(1)}, u32[]{:S(2)}, u32[]{:S(2)}) %all-to-all-start.10) | async-done | bytes 65568 | tf_op jit(solution)/shard_map/all_to_all | solution.py:53
  258.1 2.9 all-to-all-start.9
  264.2 2.5 copy_multiply_fusion.3
  268.9 18.1 %all-to-all-done.9 = bf16[8,32,16,128]{3,2,0,1:T(8,128)(2,1)S(1)} async-done(((bf16[8,32,16,128]{3,2,0,1:T(8,128)(2,1)}), bf16[8,32,16,128]{3,2,0,1:T(8,128)(2,1)S(1)}, u32[]{:S(2)}, u32[]{:S(2)}) %all-to-all-start.9) | async-done | bytes 1048608 | tf_op jit(solution)/shard_map/all_to_all | solution.py:33
  287.0 3.0 fusion.27
  290.7 12.5 %all_to_all.60 = bf16[8,8,1,2048]{3,1,2,0:T(8,128)(2,1)S(1)} all-to-all(bf16[8,8,1,2048]{3,1,2,0:T(8,128)(2,1)S(1)} %constant_dynamic-update-slice_fusion.24), channel_id=1, replica_groups=mesh['gx'=8,'gy'=4] {'gx'}, dimensions={0} | all-to-all | bytes 524288 | tf_op jit(solution)/shard_map/all_to_all | solution.py:69
  (166 shorter events, 67.5 us)
Async XLA Ops:
  51.4 10.0 %all-to-all-start.1 = ((bf16[8,32,1,128]{3,0,2,1:T(8,128)(2,1)}), bf16[8,32,1,128]{3,0,2,1:T(8,128)(2,1)S(1)}, u32[]{:S(2)}, u32[]{:S(2)}) async-start(bf16[8,32,1,128]{3,0,2,1:T(8,128)(2,1)} %select_bitcast_fusion.3), calls=%async_computation.1 | async-start | bytes 131072 | tf_op jit(solution)/shard_map/all_to_all | solution.py:53
  56.2 14.9 %copy-start.4 = (f32[4,1,16,128]{3,2,1,0:T(8,128)S(1)}, f32[4,1,16,128]{3,2,1,0:T(8,128)}, u32[]{:S(2)}) copy-start(f32[4,1,16,128]{3,2,1,0:T(8,128)} %param.17) | copy-start | bytes 98308
  61.4 31.9 %all-to-all-start = ((bf16[8,32,16,128]{3,2,0,1:T(8,128)(2,1)}), bf16[8,32,16,128]{3,2,0,1:T(8,128)(2,1)S(1)}, u32[]{:S(2)}, u32[]{:S(2)}) async-start(bf16[8,32,16,128]{3,2,0,1:T(8,128)(2,1)} %copy.483), calls=%async_computation | async-start | bytes 2097152 | tf_op jit(solution)/shard_map/all_to_all | solution.py:33
  82.5 2.0 copy-start.1
  102.0 12.8 %all-to-all-start.2 = ((bf16[8,8,1,2048]{3,1,2,0:T(8,128)(2,1)}), bf16[8,8,1,2048]{3,1,2,0:T(8,128)(2,1)S(1)}, u32[]{:S(2)}, u32[]{:S(2)}) async-start(bf16[8,8,1,2048]{3,1,2,0:T(8,128)(2,1)} %constant_dynamic-update-slice_fusion), calls=%async_computation.2 | async-start | bytes 524288 | tf_op jit(solution)/shard_map/all_to_all | solution.py:69
  115.0 17.0 %copy-start.5 = (s32[4,1,16]{2,1,0:T(1,128)S(1)}, s32[4,1,16]{2,1,0:T(1,128)}, u32[]{:S(2)}) copy-start(s32[4,1,16]{2,1,0:T(1,128)} %param.15) | copy-start | bytes 772
  118.1 11.0 %all-to-all-start.4 = ((bf16[8,32,1,128]{3,0,2,1:T(8,128)(2,1)}), bf16[8,32,1,128]{3,0,2,1:T(8,128)(2,1)S(1)}, u32[]{:S(2)}, u32[]{:S(2)}) async-start(bf16[8,32,1,128]{3,0,2,1:T(8,128)(2,1)} %select_bitcast_fusion.2), calls=%async_computation.4 | async-start | bytes 131072 | tf_op jit(solution)/shard_map/all_to_all | solution.py:53
  129.1 28.8 %all-to-all-start.3 = ((bf16[8,32,16,128]{3,2,0,1:T(8,128)(2,1)}), bf16[8,32,16,128]{3,2,0,1:T(8,128)(2,1)S(1)}, u32[]{:S(2)}, u32[]{:S(2)}) async-start(bf16[8,32,16,128]{3,2,0,1:T(8,128)(2,1)} %copy.494), calls=%async_computation.3 | async-start | bytes 2097152 | tf_op jit(solution)/shard_map/all_to_all | solution.py:33
  138.9 2.0 copy-start.2
  166.6 12.7 %all-to-all-start.5 = ((bf16[8,8,1,2048]{3,1,2,0:T(8,128)(2,1)}), bf16[8,8,1,2048]{3,1,2,0:T(8,128)(2,1)S(1)}, u32[]{:S(2)}, u32[]{:S(2)}) async-start(bf16[8,8,1,2048]{3,1,2,0:T(8,128)(2,1)} %constant_dynamic-update-slice_fusion.8), calls=%async_computation.5 | async-start | bytes 524288 | tf_op jit(solution)/shard_map/all_to_all | solution.py:69
  182.6 11.0 %all-to-all-start.7 = ((bf16[8,32,1,128]{3,0,2,1:T(8,128)(2,1)}), bf16[8,32,1,128]{3,0,2,1:T(8,128)(2,1)S(1)}, u32[]{:S(2)}, u32[]{:S(2)}) async-start(bf16[8,32,1,128]{3,0,2,1:T(8,128)(2,1)} %select_bitcast_fusion.1), calls=%async_computation.7 | async-start | bytes 131072 | tf_op jit(solution)/shard_map/all_to_all | solution.py:53
  193.6 28.8 %all-to-all-start.6 = ((bf16[8,32,16,128]{3,2,0,1:T(8,128)(2,1)}), bf16[8,32,16,128]{3,2,0,1:T(8,128)(2,1)S(1)}, u32[]{:S(2)}, u32[]{:S(2)}) async-start(bf16[8,32,16,128]{3,2,0,1:T(8,128)(2,1)} %copy.504), calls=%async_computation.6 | async-start | bytes 2097152 | tf_op jit(solution)/shard_map/all_to_all | solution.py:33
  203.1 2.0 copy-start.3
  231.1 12.7 %all-to-all-start.8 = ((bf16[8,8,1,2048]{3,1,2,0:T(8,128)(2,1)}), bf16[8,8,1,2048]{3,1,2,0:T(8,128)(2,1)S(1)}, u32[]{:S(2)}, u32[]{:S(2)}) async-start(bf16[8,8,1,2048]{3,1,2,0:T(8,128)(2,1)} %constant_dynamic-update-slice_fusion.16), calls=%async_computation.8 | async-start | bytes 524288 | tf_op jit(solution)/shard_map/all_to_all | solution.py:69
  247.1 11.0 %all-to-all-start.10 = ((bf16[8,32,1,128]{3,0,2,1:T(8,128)(2,1)}), bf16[8,32,1,128]{3,0,2,1:T(8,128)(2,1)S(1)}, u32[]{:S(2)}, u32[]{:S(2)}) async-start(bf16[8,32,1,128]{3,0,2,1:T(8,128)(2,1)} %select_bitcast_fusion), calls=%async_computation.10 | async-start | bytes 131072 | tf_op jit(solution)/shard_map/all_to_all | solution.py:53
  258.1 28.8 %all-to-all-start.9 = ((bf16[8,32,16,128]{3,2,0,1:T(8,128)(2,1)}), bf16[8,32,16,128]{3,2,0,1:T(8,128)(2,1)S(1)}, u32[]{:S(2)}, u32[]{:S(2)}) async-start(bf16[8,32,16,128]{3,2,0,1:T(8,128)(2,1)} %copy.514), calls=%async_computation.9 | async-start | bytes 2097152 | tf_op jit(solution)/shard_map/all_to_all | solution.py:33
  266.8 1.9 copy-start
